TPU v7x, 32 devices: a whole 2x2x4 slice. The times are simulated.
32 devices in a mesh: val: 4 (over x, core), cond: 8 (over z, y).
Axes of the slice: x: 2, y: 2, z: 4, core: 2. Of those that a mesh axis runs over, the one named last changes fastest.
Arguments:
- val_orbitals: bfloat16 [16, 768], P('val'), may hold values from -6 to 6
- cond_orbitals: bfloat16 [64, 768], P('cond'), may hold values from -6 to 6
- val_energy: bfloat16 [16], P('val'), may hold values from -0.59765625 to -0.049804688
- cond_energy: bfloat16 [64], P('cond'), may hold values from 0.049804688 to 1.1953125
- wave_index: int32 [4096], P('cond'), may hold values from 0 to 884735
Outputs:
- chi_real: float32 [128, 4096], P('val', 'cond')
- chi_imag: float32 [128, 4096], P('val', 'cond')
Inputs may be any that keep to these rules, and one draw needn't show every extreme that they name: `wave_index`: values may repeat.
All inputs are finite; a program needn't handle non-finite values.
Results may differ from a plain program's by a relative error of at most 0.0037.
Values may be sent and summed in bfloat16 or wider, within the bound.
A program may use at most 64 MiB of HBM per device.

v0:
```python
import math
import jax
import jax.numpy as jnp
from jax import lax
from jax.sharding import PartitionSpec as P

NG = 96
NW = 128
VB = 4
CB = 8
SLAB_Y = 4
NPTS = 768


def from_root(value, axis, source):
    kept = jnp.where(lax.axis_index(axis) == source, value, 0).astype(value.dtype)
    return lax.psum(kept, axis)


def phase_table(wave_index, point_count, grid_cells, slab_rows):
    points = lax.iota(jnp.int32, point_count)
    along_x = points % grid_cells
    along_y = points // grid_cells % slab_rows
    along_z = points // (grid_cells * slab_rows)
    wave_x = wave_index // (grid_cells * grid_cells)
    wave_y = wave_index // grid_cells % grid_cells
    wave_z = wave_index % grid_cells
    phase_turns = (
        along_x[:, None] * wave_x[None, :]
        + along_y[:, None] * wave_y[None, :]
        + along_z[:, None] * wave_z[None, :]
    ) % grid_cells
    angles = phase_turns.astype(jnp.float32) * (2.0 * math.pi / grid_cells)
    return jnp.concatenate([jnp.cos(angles), jnp.sin(angles)], axis=1).astype(jnp.bfloat16)


def pair_density(valence, conduction):
    product = conduction[:, None, :].astype(jnp.float32) * valence[None, :, :].astype(jnp.float32)
    return product.reshape(-1, valence.shape[1]).astype(jnp.bfloat16)


def pair_weights(val_energy, cond_energy):
    spread = cond_energy[:, None].astype(jnp.float32) - val_energy[None, :].astype(jnp.float32)
    return (1.0 / spread).reshape(-1)


def per_device(val_orbitals, cond_orbitals, val_energy, cond_energy, wave_index):
    window_index = from_root(wave_index[:NW], "cond", 0)
    row_table = phase_table(wave_index, NPTS, NG, SLAB_Y)
    window_table = phase_table(window_index, NPTS, NG, SLAB_Y)
    row_count = wave_index.shape[0]
    factor = -4.0 / math.sqrt(VB * lax.axis_size("val") * CB * lax.axis_size("cond"))
    conduction = lax.all_gather(cond_orbitals, "cond", axis=0, tiled=True)
    energy = lax.all_gather(cond_energy, "cond", axis=0, tiled=True)
    density = pair_density(val_orbitals, conduction)
    weights = pair_weights(val_energy, energy)
    window_terms = jnp.dot(density, window_table, preferred_element_type=jnp.float32)
    weighted = window_terms * weights[:, None]
    row_terms = jnp.dot(density, row_table, preferred_element_type=jnp.float32)
    update = jnp.dot(weighted.T, row_terms, precision=lax.Precision.HIGHEST)
    real_part = factor * (update[:NW, :row_count] + update[NW:, row_count:])
    imag_part = factor * (update[:NW, row_count:] - update[NW:, :row_count])
    return (
        lax.psum_scatter(real_part, "val", scatter_dimension=0, tiled=True),
        lax.psum_scatter(imag_part, "val", scatter_dimension=0, tiled=True),
    )


def solution(mesh):
    return jax.shard_map(
        per_device,
        mesh=mesh,
        in_specs=(P("val", None), P("cond", None), P("val"), P("cond"), P("cond")),
        out_specs=(P("val", "cond"), P("val", "cond")),
        check_vma=False,
    )
```

profile of v0, /device:TPU:0, one launch (start us, length us, event | category | flops | bytes accessed | tf_op | source)
XLA Modules:
  0.0 136.0 jit_solution(9349194043771805298)
XLA Ops:
  7.2 0.0 reduce-scatter.5.cloned.1.call-start
  7.3 0.7 add_select_fusion.9
  8.0 0.7 broadcast_select_fusion
  8.7 13.1 %psum.7 = s32[128]{0:T(128)S(1)} all-reduce(s32[128]{0:T(128)S(1)} %broadcast_select_fusion), channel_id=1, replica_groups=mesh['val'=4,'cond'=8] {'cond'}, use_global_device_ids=true, to_apply=%region_0.1 | all-reduce | flops 128 | bytes 1024 | tf_op jit(solution)/shard_map/psum | solution.py:17
  21.7 0.7 convert_element_type.36
  22.4 1.2 dynamic-slice
  24.3 0.9 dynamic-update-slice
  25.2 18.6 %all-reduce = bf16[64]{0:T(256)(128)(2,1)S(1)} all-reduce(bf16[64]{0:T(256)(128)(2,1)S(1)} %dynamic-update-slice), channel_id=1, replica_groups=mesh['val'=4,'cond'=8] {'cond'}, use_global_device_ids=true, to_apply=%add | all-reduce | flops 64 | bytes 256
  43.8 0.7 convert_element_type.31
  44.5 0.1 subtract_divide_fusion
  44.6 0.1 div.65
  44.7 30.8 %all_gather.6 = bf16[64,768]{1,0:T(8,128)(2,1)S(1)} all-gather(bf16[8,768]{1,0:T(8,128)(2,1)} %param.6), channel_id=1, replica_groups=mesh['val'=4,'cond'=8] {'cond'}, dimensions={0}, use_global_device_ids=true | all-gather | bytes 110592 | tf_op jit(solution)/shard_map/all_gather | solution.py:53
  75.5 0.1 multiply_convert_fusion
  75.6 0.1 convert_element_type.33
  75.7 2.4 %cosine_convert_fusion.1 = (bf16[768,128]{1,0:T(8,128)(2,1)S(1)}, bf16[768,128]{1,0:T(8,128)(2,1)S(1)}) fusion(s32[128]{0:T(128)S(1)} %get-tuple-element.13, s32[768]{0:T(1024)S(1)} %get-tuple-element.14, s32[128]{0:T(128)S(1)} %get-tuple-element.12, s32[768]{0:T(1024)S(1)} %get-tuple-element.15, s32[128]{0:T(128)S(1)} %get-tuple-element.11, ...), kind=kLoop, calls=%fused_computation.22 | loop fusion | flops 1474560 | bytes 403968 | tf_op jit(solution)/shard_map/convert.2
  78.1 7.6 %cosine_convert_fusion = (bf16[768,512]{1,0:T(8,128)(2,1)S(1)}, bf16[768,512]{1,0:T(8,128)(2,1)S(1)}) fusion(s32[512]{0:T(512)S(1)} %get-tuple-element.10, s32[768]{0:T(1024)S(1)} %get-tuple-element.14, s32[512]{0:T(512)S(1)} %get-tuple-element.9, s32[768]{0:T(1024)S(1)} %get-tuple-element.15, s32[512]{0:T(512)S(1)} %get-tuple-element.8, ...), kind=kLoop, calls=%fused_computation.8 | loop fusion | flops 5898240 | bytes 1588224 | tf_op jit(solution)/shard_map/convert
  85.7 0.6 fusion.2
  86.3 0.3 convolution_multiply_fusion
  86.6 1.0 fusion.31
  87.6 0.9 fusion.17
  88.5 0.0 reduce-scatter.3.cloned.1.call-start
  88.6 0.7 reduce-scatter.3.cloned.1.call-update
  89.3 16.7 %reduce-scatter.5.cloned.1.call-done = f32[32,512]{1,0:T(8,128)} async-done(((f32[128,512]{1,0:T(8,128)}), f32[32,512]{1,0:T(8,128)}) %reduce-scatter.5.cloned.1.call-update) | async-done | bytes 65552 | tf_op jit(solution)/shard_map/reduce_scatter | solution.py:65
  106.0 23.1 %reduce-scatter.3.cloned.1.call-done = f32[32,512]{1,0:T(8,128)} async-done(((f32[128,512]{1,0:T(8,128)}), f32[32,512]{1,0:T(8,128)}) %reduce-scatter.3.cloned.1.call-update) | async-done | bytes 65552 | tf_op jit(solution)/shard_map/reduce_scatter | solution.py:64
  (7 shorter events, 0.1 us)
Async XLA Ops:
  7.2 98.8 %reduce-scatter.5.cloned.1.call-start = ((), (), s32[]{:S(2)}) async-start(), calls=%async_computation.3 | async-start | bytes 327680 | tf_op jit(solution)/shard_map/reduce_scatter | solution.py:65
  88.5 40.6 %reduce-scatter.3.cloned.1.call-start = ((), (), s32[]{:S(2)}) async-start(), calls=%async_computation.2 | async-start | bytes 327680 | tf_op jit(solution)/shard_map/reduce_scatter | solution.py:64
Sparse Core Ops, SparseCore 0:
  88.7 17.3 reduce-scatter.4
  109.0 20.0 reduce-scatter.2
where the time goes:
time: 136 us
  blocking collectives  62.5 us (46%)
  waiting for transfers between devices  40.6 us (30%)
  between operations  14.8 us (11%)
  other arithmetic  13.9 us (10%)
  local copies, waits for them, and re-layouts  2.3 us (2%)
  matrix products  1.87 us (1%)
    all_gather x1, blocking collectives, per_device(): conduction = lax.all_gather(cond_orbitals, 'cond', axis=0, tiled=True)  30.8 us
    reduce_scatter x1, waiting for transfers between devices, per_device(): lax.psum_scatter(real_part, 'val', scatter_dimension=0, tiled=True)  23.1 us
    unnamed x1, blocking collectives  18.6 us
    reduce_scatter x1, waiting for transfers between devices, per_device(): lax.psum_scatter(imag_part, 'val', scatter_dimension=0, tiled=True)  16.7 us
    psum x1, blocking collectives, from_root(): return lax.psum(kept, axis)  13.1 us
    another operation x2, other arithmetic  10 us
  transfers between devices with their start and end apart: 2, of which 2 were waited for; matrix products, arithmetic and copies ran while one was open for 0% of the time, Pallas kernels for 0%

commit v1 on v0

--- a/solution.py
+++ b/solution.py
@@ -14,7 +14,7 @@
 
 def from_root(value, axis, source):
     kept = jnp.where(lax.axis_index(axis) == source, value, 0).astype(value.dtype)
-    return lax.psum(kept, axis)
+    return jnp.sum(lax.all_gather(kept, axis), axis=0)
 
 
 def phase_table(wave_index, point_count, grid_cells, slab_rows):

time: 136 us -> 146 us (1.074)
  blocking collectives: 62.5 us -> 70.2 us
    all_gather x0 -> x1, blocking collectives: none -> 16.3 us  [from_root(): return jnp.sum(lax.all_gather(kept, axis), axis=0)]
    psum x1 -> x0, blocking collectives: 13.1 us -> none  [from_root(): return lax.psum(kept, axis)]
    unnamed x1, blocking collectives: 18.6 us -> 23.1 us
where the time goes in v1:
time: 146 us; the launch traced here: 145 us
  blocking collectives  70.2 us (48%)
  waiting for transfers between devices  42 us (29%)
  between operations  14.8 us (10%)
  other arithmetic  13.9 us (10%)
  local copies, waits for them, and re-layouts  2.3 us (2%)
  matrix products  1.88 us (1%)
    all_gather x1, blocking collectives, per_device(): conduction = lax.all_gather(cond_orbitals, 'cond', axis=0, tiled=True)  30.8 us
    unnamed x1, blocking collectives  23.1 us
    reduce_scatter x1, waiting for transfers between devices, per_device(): lax.psum_scatter(real_part, 'val', scatter_dimension=0, tiled=True)  23.1 us
    reduce_scatter x1, waiting for transfers between devices, per_device(): lax.psum_scatter(imag_part, 'val', scatter_dimension=0, tiled=True)  18.2 us
    all_gather x1, blocking collectives, from_root(): return jnp.sum(lax.all_gather(kept, axis), axis=0)  16.3 us
    another operation x2, other arithmetic  10 us
  transfers between devices with their start and end apart: 2, of which 2 were waited for; matrix products, arithmetic and copies ran while one was open for 0% of the time, Pallas kernels for 0%

profile of v1, /device:TPU:0, one launch (start us, length us, event | category | flops | bytes accessed | tf_op | source)
XLA Modules:
  0.0 145.2 jit_solution(2869890248730439564)
XLA Ops:
  7.2 0.0 reduce-scatter.5.cloned.1.call-start
  7.3 0.7 add_select_fusion.9
  8.0 0.7 fusion.29
  8.7 0.7 convert_element_type.36
  9.3 1.2 dynamic-slice
  11.2 0.9 dynamic-update-slice
  12.1 23.1 %all-reduce = bf16[64]{0:T(256)(128)(2,1)S(1)} all-reduce(bf16[64]{0:T(256)(128)(2,1)S(1)} %dynamic-update-slice), channel_id=1, replica_groups=mesh['val'=4,'cond'=8] {'cond'}, use_global_device_ids=true, to_apply=%add | all-reduce | flops 64 | bytes 256
  35.2 16.3 %all-gather.1 = s32[8,1,128]{2,1,0:T(1,128)S(1)} all-gather(s32[1,1,128]{2,1,0:T(1,128)S(1)} %fusion.29), channel_id=2, replica_groups=mesh['val'=4,'cond'=8] {'cond'}, dimensions={0}, use_global_device_ids=true | all-gather | bytes 4608 | tf_op jit(solution)/shard_map/all_gather | solution.py:17
  51.5 0.7 convert_element_type.31
  52.2 0.1 subtract_divide_fusion
  52.3 0.1 div.73
  52.4 30.8 %all_gather.12 = bf16[64,768]{1,0:T(8,128)(2,1)S(1)} all-gather(bf16[8,768]{1,0:T(8,128)(2,1)} %param.6), channel_id=1, replica_groups=mesh['val'=4,'cond'=8] {'cond'}, dimensions={0}, use_global_device_ids=true | all-gather | bytes 110592 | tf_op jit(solution)/shard_map/all_gather | solution.py:53
  83.2 0.1 multiply_convert_fusion
  83.4 0.1 convert_element_type.33
  83.5 2.4 %cosine_convert_fusion.1 = (bf16[768,128]{1,0:T(8,128)(2,1)S(1)}, bf16[768,128]{1,0:T(8,128)(2,1)S(1)}) fusion(s32[128]{0:T(128)S(1)} %get-tuple-element.13, s32[768]{0:T(1024)S(1)} %get-tuple-element.14, s32[128]{0:T(128)S(1)} %get-tuple-element.12, s32[768]{0:T(1024)S(1)} %get-tuple-element.15, s32[128]{0:T(128)S(1)} %get-tuple-element.11, ...), kind=kLoop, calls=%fused_computation.22 | loop fusion | flops 1474560 | bytes 403968 | tf_op jit(solution)/shard_map/convert.2
  85.8 7.6 %cosine_convert_fusion = (bf16[768,512]{1,0:T(8,128)(2,1)S(1)}, bf16[768,512]{1,0:T(8,128)(2,1)S(1)}) fusion(s32[512]{0:T(512)S(1)} %get-tuple-element.10, s32[768]{0:T(1024)S(1)} %get-tuple-element.14, s32[512]{0:T(512)S(1)} %get-tuple-element.9, s32[768]{0:T(1024)S(1)} %get-tuple-element.15, s32[512]{0:T(512)S(1)} %get-tuple-element.8, ...), kind=kLoop, calls=%fused_computation.8 | loop fusion | flops 5898240 | bytes 1588224 | tf_op jit(solution)/shard_map/convert
  93.5 0.6 fusion.2
  94.0 0.3 convolution_multiply_fusion
  94.3 1.0 fusion.32
  95.4 0.9 fusion.17
  96.3 0.0 reduce-scatter.3.cloned.1.call-start
  96.3 0.7 reduce-scatter.3.cloned.1.call-update
  97.0 18.2 %reduce-scatter.5.cloned.1.call-done = f32[32,512]{1,0:T(8,128)} async-done(((f32[128,512]{1,0:T(8,128)}), f32[32,512]{1,0:T(8,128)}) %reduce-scatter.5.cloned.1.call-update) | async-done | bytes 65552 | tf_op jit(solution)/shard_map/reduce_scatter | solution.py:65
  115.2 23.1 %reduce-scatter.3.cloned.1.call-done = f32[32,512]{1,0:T(8,128)} async-done(((f32[128,512]{1,0:T(8,128)}), f32[32,512]{1,0:T(8,128)}) %reduce-scatter.3.cloned.1.call-update) | async-done | bytes 65552 | tf_op jit(solution)/shard_map/reduce_scatter | solution.py:64
  (8 shorter events, 0.1 us)
Async XLA Ops:
  7.2 108.0 %reduce-scatter.5.cloned.1.call-start = ((), (), s32[]{:S(2)}) async-start(), calls=%async_computation.3 | async-start | bytes 327680 | tf_op jit(solution)/shard_map/reduce_scatter | solution.py:65
  96.3 42.1 %reduce-scatter.3.cloned.1.call-start = ((), (), s32[]{:S(2)}) async-start(), calls=%async_computation.2 | async-start | bytes 327680 | tf_op jit(solution)/shard_map/reduce_scatter | solution.py:64
Sparse Core Ops, SparseCore 0:
  96.4 18.7 reduce-scatter.4
  118.2 20.0 reduce-scatter.2
